TPU v7x, 32 devices: a whole 2x2x4 slice. The times are simulated.
32 devices in a mesh: ctx: 8 (over z, core), head: 4 (over y, x).
Axes of the slice: x: 2, y: 2, z: 4, core: 2. Of those that a mesh axis runs over, the one named last changes fastest.
Arguments:
- query: bfloat16 [4096, 64, 128], P('ctx', 'head'), may hold values from -8 to 8
- keys: bfloat16 [4096, 8, 128], P('ctx', 'head'), may hold values from -8 to 8
- values: bfloat16 [4096, 8, 128], P('ctx', 'head'), may hold values from -6 to 6
- k_scale: bfloat16 [16, 8], P('ctx', 'head'), may hold values from 0.59765625 to 1.59375
- v_scale: bfloat16 [16, 8], P('ctx', 'head'), may hold values from 0.5 to 2
- block_place: int32 [16], P('ctx'), may hold values from 0 to 15, as said below
- out_weight: bfloat16 [8192, 8192], P('head'), may hold values from -1 to 1
Outputs:
- mixed: bfloat16 [4096, 8192], P(('ctx', 'head'))
Inputs may be any that keep to these rules, and one draw needn't show every extreme that they name: `block_place`: A permutation of the block indices in which entries 2r and 2r + 1 sum to 15 and entry 2r is below 8.
All inputs are finite; a program needn't handle non-finite values.
Results may differ from a plain program's by a relative error of at most 0.015.
Values may be sent and summed in bfloat16 or wider, within the bound.
A program may use at most 128 MiB of HBM per device.

v0:
```python
import functools
import math

import jax
import jax.numpy as jnp
from jax import lax
from jax.experimental import pallas as pl
from jax.experimental.pallas import tpu as pltpu
from jax.sharding import PartitionSpec as P

masked_value = -1e30
COLUMN_STEP = 512
LAG = 3


def attend_kernel(
    per_group, block_len, head_dim, blocks, first_slot, later,
    order, own, key_gain, value_gain,
    q_ref, k_ref, vt_ref, *refs,
):
    group = pl.program_id(0)
    query_ref = refs[-1]
    if later:
        old_max, old_total, old_sum, o_ref, max_ref, total_ref, sum_ref = refs[:-1]
    elif first_slot == 0:
        o_ref, max_ref, total_ref, sum_ref = refs[:-1]
    else:
        max_ref, total_ref, sum_ref = refs[:-1]
    place = own[first_slot]
    for h in range(per_group):
        query_ref[h] = q_ref[:, h * head_dim : (h + 1) * head_dim].T

    def visit(indices, diagonal):
        found = [order[index] for index in indices]
        keys = [k_ref[lax.div(block, 2)] for block in found]
        values = [vt_ref[lax.div(block, 2)] for block in found]
        gains = [key_gain[group * blocks + block] for block in found]
        scales = [value_gain[group * blocks + block] for block in found]
        if diagonal:
            shape = (block_len, block_len)
            visible = lax.broadcasted_iota(jnp.int32, shape, 0) <= lax.broadcasted_iota(
                jnp.int32, shape, 1
            )

        def score(h):
            result = [
                jnp.dot(key, query_ref[h], preferred_element_type=jnp.float32) for key in keys
            ]
            if diagonal:
                result[-1] = jnp.where(visible, result[-1], masked_value)
            return result

        def weigh(h, scores):
            old = max_ref[h : h + 1, :]
            top = old
            for part, gain in zip(scores, gains):
                top = jnp.maximum(top, jnp.max(part, axis=0, keepdims=True) * gain)
            factor = jnp.exp2(old - top)
            total = factor * total_ref[h : h + 1, :]
            rounded = []
            for part, gain in zip(scores, gains):
                weights = jnp.exp2(part * gain - top)
                total = total + jnp.sum(weights, axis=0, keepdims=True)
                rounded.append(weights.astype(jnp.bfloat16))
            max_ref[h : h + 1, :] = top
            total_ref[h : h + 1, :] = total
            return rounded, factor

        def gather(h, rounded, factor):
            running = factor * sum_ref[h]
            for part, value, scale in zip(rounded, values, scales):
                running = running + scale * jnp.dot(
                    value, part, preferred_element_type=jnp.float32
                )
            sum_ref[h] = running

        scores = score(0)
        waiting = None
        for h in range(per_group):
            upcoming = score(h + 1) if h + 1 < per_group else None
            if waiting is not None:
                gather(h - 1, *waiting)
            waiting = weigh(h, scores)
            scores = upcoming
        gather(per_group - 1, *waiting)

    half = blocks // 2
    if later:
        max_ref[...] = old_max[...]
        total_ref[...] = old_total[...]
        sum_ref[...] = old_sum[...]
        start, stop = half, place
    else:
        max_ref[...] = jnp.full(max_ref.shape, masked_value, jnp.float32)
        total_ref[...] = jnp.zeros(total_ref.shape, jnp.float32)
        sum_ref[...] = jnp.zeros(sum_ref.shape, jnp.float32)
        start, stop = 0, (place if first_slot == 0 else half)
    pairs = (stop - start) // 2

    @pl.loop(0, pairs)
    def _(pair):
        visit([start + 2 * pair, start + 2 * pair + 1], False)

    if later or first_slot == 0:
        odd = (stop - start) - 2 * pairs

        @pl.when(odd == 1)
        def _():
            visit([place - 1, place], True)

        @pl.when(odd == 0)
        def _():
            visit([place], True)

        for h in range(per_group):
            columns = slice(h * head_dim, (h + 1) * head_dim)
            mean = sum_ref[h] / total_ref[h : h + 1, :]
            o_ref[:, columns] = mean.T.astype(o_ref.dtype)
    elif half % 2:
        visit([half - 1], False)


def attend(facts, query, gathered, group_count, head_dim, slot, state=None):
    rows, width = query.shape
    devices = gathered.shape[0]
    block_len = rows // 2
    group_width = width // group_count
    per_group = group_width // head_dim
    heads = group_count * per_group
    blocks = facts[0].shape[0]
    later = state is not None
    tiles = blocks // 4 if later or slot == 0 else blocks // 2
    pairs = tiles * block_len * block_len * heads
    row_spec = pl.BlockSpec((per_group, block_len), lambda g, *_: (g, 0))
    sum_spec = pl.BlockSpec((per_group, head_dim, block_len), lambda g, *_: (g, 0, 0))
    state_specs = [row_spec, row_spec, sum_spec]
    row_shape = (per_group, block_len)
    sum_shape = (per_group, head_dim, block_len)
    first_value = block_len // head_dim
    outs = ([pl.BlockSpec((block_len, group_width), lambda g, *_: (0, g))],
            [jax.ShapeDtypeStruct((block_len, width), jnp.bfloat16)])
    scratch = [
        pltpu.VMEM(row_shape, jnp.float32),
        pltpu.VMEM(row_shape, jnp.float32),
        pltpu.VMEM(sum_shape, jnp.float32),
    ]
    if not later and slot == 1:
        outs = (state_specs, [
            jax.ShapeDtypeStruct((heads, block_len), jnp.float32),
            jax.ShapeDtypeStruct((heads, block_len), jnp.float32),
            jax.ShapeDtypeStruct((heads, head_dim, block_len), jnp.float32),
        ])
        scratch = []
    scratch.append(pltpu.VMEM((per_group, head_dim, block_len), jnp.bfloat16))
    results = pl.pallas_call(
        functools.partial(
            attend_kernel, per_group, block_len, head_dim, blocks, slot, later
        ),
        grid_spec=pltpu.PrefetchScalarGridSpec(
            num_scalar_prefetch=4,
            grid=(group_count,),
            in_specs=[
                pl.BlockSpec((block_len, group_width), lambda g, *_: (slot, g)),
                pl.BlockSpec((devices, block_len, head_dim), lambda g, *_: (0, 0, g)),
                pl.BlockSpec(
                    (devices, head_dim, block_len), lambda g, *_: (0, first_value + g, 0)
                ),
            ] + (state_specs if later else []),
            out_specs=outs[0],
            scratch_shapes=scratch,
        ),
        out_shape=outs[1],
        compiler_params=pltpu.CompilerParams(vmem_limit_bytes=40 * 1024 * 1024),
        cost_estimate=pl.CostEstimate(
            flops=4 * pairs * head_dim, bytes_accessed=4 << 20, transcendentals=pairs
        ),
    )(*facts, query, gathered, gathered, *(state if later else ()))
    return results if len(results) > 1 else results[0]


def project_kernel(
    chunks,
    low_ref, high_ref, w_ref, o_ref,
    lhs, sent, kept, arrived, passed, ended,
    send_one, recv_one, send_two, recv_two,
):
    t = pl.program_id(0)
    me = lax.axis_index("head")
    along_x = me + 1 - 2 * (me % 2)
    along_y = (me + 2) % 4
    part = low_ref.shape[0] // 2

    @pl.when(t == 0)
    def _():
        barrier = pltpu.get_barrier_semaphore()
        for partner in (along_x, along_y):
            pl.semaphore_signal(
                barrier, inc=1, device_id={"head": partner},
                device_id_type=pl.DeviceIdType.MESH,
            )
        for parity in range(2):
            near, far = (along_x, along_y) if parity == 0 else (along_y, along_x)
            for slot, owner in enumerate((3 - me, near, far, me)):
                rows = pl.ds(pl.multiple_of((owner % 2) * part, part), part)

                @pl.when(owner // 2 == 0)
                def _():
                    lhs[parity, slot * part : (slot + 1) * part, :] = low_ref[rows, :]

                @pl.when(owner // 2 == 1)
                def _():
                    lhs[parity, slot * part : (slot + 1) * part, :] = high_ref[rows, :]

        pl.semaphore_wait(barrier, 2)

    def first_copy(c):
        near = along_x + (c % 2) * (along_y - along_x)
        return pltpu.make_async_remote_copy(
            src_ref=sent.at[c], dst_ref=arrived.at[c],
            send_sem=send_one.at[c], recv_sem=recv_one.at[c],
            device_id={"head": near}, device_id_type=pl.DeviceIdType.MESH,
        )

    def second_copy(c):
        far = along_y + (c % 2) * (along_x - along_y)
        return pltpu.make_async_remote_copy(
            src_ref=passed.at[c], dst_ref=ended.at[c],
            send_sem=send_two.at[c], recv_sem=recv_two.at[c],
            device_id={"head": far}, device_id_type=pl.DeviceIdType.MESH,
        )

    @pl.when(t < chunks)
    def _():
        term = jnp.dot(lhs[t % 2], w_ref[...], preferred_element_type=jnp.float32)
        term = term.astype(jnp.bfloat16)
        sent[t] = term[: 2 * part]
        kept[t] = term[2 * part :]
        first_copy(t).start()

    @pl.when((t >= LAG) & (t < chunks + LAG))
    def _():
        c = t - LAG
        first_copy(c).wait()
        passed[c] = (
            arrived[c, :part, :].astype(jnp.float32) + kept[c, :part, :].astype(jnp.float32)
        ).astype(jnp.bfloat16)
        second_copy(c).start()

    @pl.when(t >= 2 * LAG)
    def _():
        c = t - 2 * LAG
        second_copy(c).wait()
        o_ref[...] = (
            arrived[c, part:, :].astype(jnp.float32)
            + kept[c, part:, :].astype(jnp.float32)
            + ended[c].astype(jnp.float32)
        ).astype(jnp.bfloat16)


def project(low, high, weight):
    depth, columns = weight.shape
    rows = 2 * low.shape[0]
    part = rows // 4
    step = COLUMN_STEP
    chunks = columns // step
    last = chunks - 1
    return pl.pallas_call(
        functools.partial(project_kernel, chunks),
        grid_spec=pltpu.PrefetchScalarGridSpec(
            num_scalar_prefetch=0,
            grid=(chunks + 2 * LAG,),
            in_specs=[
                pl.BlockSpec((rows // 2, depth), lambda t: (0, 0)),
                pl.BlockSpec((rows // 2, depth), lambda t: (0, 0)),
                pl.BlockSpec((depth, step), lambda t: (0, jnp.minimum(t, last))),
            ],
            out_specs=pl.BlockSpec((part, step), lambda t: (0, jnp.maximum(t - 2 * LAG, 0))),
            scratch_shapes=[
                pltpu.VMEM((2, rows, depth), jnp.bfloat16),
                pltpu.VMEM((chunks, 2 * part, step), jnp.bfloat16),
                pltpu.VMEM((chunks, 2 * part, step), jnp.bfloat16),
                pltpu.VMEM((chunks, 2 * part, step), jnp.bfloat16),
                pltpu.VMEM((chunks, part, step), jnp.bfloat16),
                pltpu.VMEM((chunks, part, step), jnp.bfloat16),
                pltpu.SemaphoreType.DMA((chunks,)),
                pltpu.SemaphoreType.DMA((chunks,)),
                pltpu.SemaphoreType.DMA((chunks,)),
                pltpu.SemaphoreType.DMA((chunks,)),
            ],
        ),
        out_shape=jax.ShapeDtypeStruct((part, columns), jnp.bfloat16),
        compiler_params=pltpu.CompilerParams(
            collective_id=0, has_side_effects=True, vmem_limit_bytes=56 * 1024 * 1024
        ),
        cost_estimate=pl.CostEstimate(
            flops=2 * rows * depth * columns, bytes_accessed=2 * depth * columns,
            transcendentals=0,
        ),
    )(low, high, weight)


def body(query, keys, values, k_scale, v_scale, block_place, out_weight):
    rows, head_count, head_dim = query.shape
    group_count = keys.shape[1]
    slots = block_place.shape[0]
    devices = lax.axis_size("ctx")
    blocks = slots * devices
    block_len = rows // slots
    width = group_count * head_dim
    facts = jnp.concatenate(
        [k_scale, v_scale, block_place[:, None].astype(jnp.bfloat16)], axis=1
    )
    facts = jnp.pad(facts, ((0, 16 - slots), (0, block_len - facts.shape[1])))

    def payload(slot):
        part = slice(slot * block_len, (slot + 1) * block_len)
        key = keys[part].reshape(block_len, width)
        key = jnp.pad(key, ((0, 0), (0, block_len - width))) if width < block_len else key
        return [key, values[part].reshape(block_len, width).T]

    low_part = lax.all_gather(jnp.concatenate(payload(0) + [facts]), "ctx", axis=0)
    high_part = lax.all_gather(jnp.concatenate(payload(1)), "ctx", axis=0)
    base = block_len + width
    all_facts = low_part[:, base : base + slots, : 2 * group_count + 1].reshape(blocks, -1)
    all_facts = all_facts.astype(jnp.float32)
    places = all_facts[:, -1].astype(jnp.int32)
    ids = jnp.arange(blocks, dtype=jnp.int32)
    order = jnp.sum(jnp.where(places[None, :] == ids[:, None], ids[None, :], 0), axis=1)
    rate = math.log2(math.e) / math.sqrt(head_dim)
    key_gain = (all_facts[:, :group_count] * rate).T.reshape(-1)
    value_gain = all_facts[:, group_count : 2 * group_count].T.reshape(-1)
    known = (order, block_place, key_gain, value_gain)
    flat = query.reshape(rows, head_count * head_dim)
    state = attend(known, flat, low_part, group_count, head_dim, 1)
    low = attend(known, flat, low_part, group_count, head_dim, 0)
    high = attend(known, flat, high_part, group_count, head_dim, 1, state)
    if lax.axis_size("head") == 4:
        return project(low, high, out_weight)
    term = jnp.dot(jnp.concatenate([low, high]), out_weight, preferred_element_type=jnp.float32)
    return lax.psum_scatter(
        term.astype(jnp.bfloat16), "head", scatter_dimension=0, tiled=True
    )


def solution(mesh):
    placed = (
        P("ctx", "head", None),
        P("ctx", "head", None),
        P("ctx", "head", None),
        P("ctx", "head"),
        P("ctx", "head"),
        P("ctx"),
        P("head", None),
    )
    return jax.shard_map(
        body, mesh=mesh, in_specs=placed, out_specs=P(("ctx", "head"), None), check_vma=False
    )
```

profile of v0, /device:TPU:0, one launch (start us, length us, event | category | flops | bytes accessed | tf_op | source)
XLA Modules:
  0.0 173.7 jit_solution(9545049793146335837)
XLA Ops:
  6.5 1.1 fusion.12
  7.7 0.1 copy.23
  7.8 1.2 fusion.11
  9.0 0.7 convert_bitcast_fusion
  9.7 0.1 copy.19
  9.8 0.7 fusion.8
  10.5 0.7 pad_maximum_fusion
  11.5 0.7 pad_maximum_fusion.1
  12.2 2.1 %copy.31 = bf16[64,8,16,128]{3,1,2,0:T(8,128)(2,1)S(1)} copy(bf16[64,8,16,128]{3,2,1,0:T(8,128)(2,1)} %bitcast.38) | data formatting | bytes 4194304
  14.4 29.4 %all-gather.5.cloned.1.call-done = bf16[4224,256]{1,0:T(8,128)(2,1)} async-done(((bf16[528,256]{1,0:T(8,128)(2,1)}), bf16[4224,256]{1,0:T(8,128)(2,1)}) %all-gather.5.cloned.1.call-update) | async-done | bytes 2162704 | tf_op jit(solution)/shard_map/all_gather | solution.py:321
  43.8 0.7 slice.32
  44.9 0.2 fusion.10
  45.1 0.1 select_reduce_fusion.order
  45.2 1.6 copy-done.5
  46.8 14.8 %shard_map.73.low_ref = bf16[256,2048]{1,0:T(8,128)(2,1)S(1)} custom-call(s32[16]{0:T(128)S(1)} %select_reduce_fusion.order, s32[2]{0:T(128)S(1)} %copy-done.4, f32[32]{0:T(128)S(1)} %reshape.33.key_gain, f32[32]{0:T(128)S(1)} %reshape.34.value_gain, bf16[512,2048]{1,0:T(8,128)(2,1)S(1)} %bitcast.28, bf16[8,528,256]{2,1,0:T(8,128)(2,1)S(1)} %bitcast.34, ...), custom_call_target="tpu_custom_call" | custom-call | flops 2147483648 | bytes 4194304 | tf_op jit(solution)/shard_map/pallas_call | solution.py:155
  61.7 1.0 copy-done.6
  62.6 14.6 %shard_map.74 = (f32[16,256]{1,0:T(8,128)S(1)}, f32[16,256]{1,0:T(8,128)S(1)}, f32[16,128,256]{2,1,0:T(8,128)S(1)}) custom-call(s32[16]{0:T(128)S(1)} %select_reduce_fusion.order, s32[2]{0:T(128)S(1)} %copy-done.4, f32[32]{0:T(128)S(1)} %reshape.33.key_gain, f32[32]{0:T(128)S(1)} %reshape.34.value_gain, bf16[512,2048]{1,0:T(8,128)(2,1)S(1)} %bitcast.29, ...), custom_call_target="tpu_custom_call" | custom-call | flops 4294967296 | bytes 4194304 | tf_op jit(solution)/shard_map/pallas_call | solution.py:155
  77.3 1.3 copy-done.1
  78.6 1.6 copy-done
  80.2 1.6 copy-done.2
  81.8 4.2 %shard_map.75.high_ref = bf16[256,2048]{1,0:T(8,128)(2,1)S(1)} custom-call(s32[16]{0:T(128)S(1)} %select_reduce_fusion.order, s32[2]{0:T(128)S(1)} %copy-done.4, f32[32]{0:T(128)S(1)} %reshape.33.key_gain, f32[32]{0:T(128)S(1)} %reshape.34.value_gain, bf16[512,2048]{1,0:T(8,128)(2,1)S(1)} %bitcast.30, bf16[8,512,256]{2,1,0:T(8,128)(2,1)S(1)} %bitcast.31, ...), custom_call_target="tpu_custom_call" | custom-call | flops 2147483648 | bytes 4194304 | tf_op jit(solution)/shard_map/pallas_call | solution.py:155
  85.9 1.0 copy-done.3
  86.9 76.8 %shard_map.76 = bf16[128,8192]{1,0:T(8,128)(2,1)} custom-call(bf16[256,2048]{1,0:T(8,128)(2,1)} %copy-done.6, bf16[256,2048]{1,0:T(8,128)(2,1)} %copy-done.3, bf16[2048,8192]{1,0:T(8,128)(2,1)} %w_ref.1), custom_call_target="tpu_custom_call" | custom-call | flops 17179869184 | bytes 33554432 | tf_op jit(solution)/shard_map/pallas_call | solution.py:267
  163.7 3.1 %copy.35 = bf16[128,8192]{1,0:T(8,128)(2,1)} copy(bf16[128,8192]{1,0:T(8,128)(2,1)} %shard_map.76) | data formatting | bytes 4194304
  (22 shorter events, 0.7 us)
Async XLA Ops:
  6.5 37.2 %all-gather.5.cloned.1.call-start = ((), (), s32[]{:S(2)}) async-start(), calls=%async_computation | async-start | bytes 2433024 | tf_op jit(solution)/shard_map/all_gather | solution.py:321
  11.3 67.3 %all-gather.7.cloned.1.call-start = ((), (), s32[]{:S(2)}) async-start(), calls=%async_computation.1 | async-start | bytes 2359296 | tf_op jit(solution)/shard_map/all_gather | solution.py:322
  12.2 33.0 %copy-start.4 = (s32[2]{0:T(128)S(1)}, s32[2]{0:T(128)}, u32[]{:S(2)}) copy-start(s32[2]{0:T(128)} %own.5) | copy-start | bytes 28
  45.2 1.6 copy-start.5
  61.7 1.0 copy-start.6
  77.2 1.3 copy-start.1
  78.6 1.6 copy-start
  80.2 1.6 copy-start.2
  85.9 1.0 copy-start.3
Sparse Core Ops, SparseCore 0:
  11.4 32.3 all-gather.4
  45.4 28.6 all-gather.6
where the time goes:
time: 176 us; the launch traced here: 174 us
  Pallas kernels  110 us (62%)
  waiting for transfers between devices  29.4 us (17%)
  local copies, waits for them, and re-layouts  17 us (10%)
  between operations  13.5 us (8%)
  other arithmetic  3.25 us (2%)
    pallas_call x1, Pallas kernels, project(): pl.pallas_call(functools.partial(project_kernel, chunks), grid_spec=pltpu...  76.8 us
    pallas_call x3, Pallas kernels, attend(): pl.pallas_call(functools.partial(attend_kernel, per_group, block_len, hea...  33.6 us
    all_gather x1, waiting for transfers between devices, body(): lax.all_gather(jnp.concatenate(payload(0) + [facts]), 'ctx', axis=0)  29.4 us
    unnamed x18, local copies, waits for them, and re-layouts  13.3 us
  transfers between devices with their start and end apart: 2, of which 1 were waited for; matrix products, arithmetic and copies ran while one was open for 3% of the time, Pallas kernels for 17%

commit v1 on v0

--- a/solution.py
+++ b/solution.py
@@ -178,6 +178,377 @@
     return results if len(results) > 1 else results[0]
 
 
+def gather_attend_kernel(
+    rate, per_group, head_dim,
+    own_ref, own_facts, q_ref, o_ref,
+    kv, facts, query_ref, max_ref, total_ref, sum_ref,
+    recv, send_right, send_left, send_beside,
+):
+    groups = kv.shape[1] // 2
+    units = kv.shape[1]
+    block_len = kv.shape[2]
+    chips = kv.shape[0] // 2
+    me = lax.axis_index("ctx")
+    z, core = me // 2, me % 2
+    beside = 2 * z + 1 - core
+    half = z // 2
+    middle = (z % 2 + half) % 2
+    first = z + 1 - 2 * (z % 2)
+    second = 2 - half
+    third = 3 * (1 - half)
+
+    barrier = pltpu.get_barrier_semaphore()
+
+    def greet(device):
+        pl.semaphore_signal(
+            barrier, inc=1, device_id={"ctx": device}, device_id_type=pl.DeviceIdType.MESH
+        )
+
+    greet(beside)
+
+    @pl.when(z > 0)
+    def _():
+        greet(me - 2)
+
+    @pl.when(z < chips - 1)
+    def _():
+        greet(me + 2)
+
+    for unit in range(units):
+        kv[me, unit] = own_ref[unit]
+    facts[me] = own_facts[...]
+
+    @pl.when((z > 0) & (z < chips - 1))
+    def _():
+        pl.semaphore_wait(barrier, 3)
+
+    @pl.when((z == 0) | (z == chips - 1))
+    def _():
+        pl.semaphore_wait(barrier, 2)
+
+    def move(origin, unit, sems, target):
+        return pltpu.make_async_remote_copy(
+            src_ref=kv.at[origin, unit], dst_ref=kv.at[origin, unit],
+            send_sem=sems.at[origin // 2, unit], recv_sem=recv.at[origin, unit],
+            device_id={"ctx": target}, device_id_type=pl.DeviceIdType.MESH,
+        )
+
+    def move_facts(origin, sems, target):
+        return pltpu.make_async_remote_copy(
+            src_ref=facts.at[origin], dst_ref=facts.at[origin],
+            send_sem=sems.at[origin // 2, units], recv_sem=recv.at[origin, units],
+            device_id={"ctx": target}, device_id_type=pl.DeviceIdType.MESH,
+        )
+
+    def send_own(sems, target):
+        move_facts(me, sems, target).start()
+        for unit in range(units):
+            move(me, unit, sems, target).start()
+
+    @pl.when(z < chips - 1)
+    def _():
+        send_own(send_right, me + 2)
+
+    @pl.when(z > 0)
+    def _():
+        send_own(send_left, me - 2)
+
+    send_own(send_beside, beside)
+
+    def on(chip, action):
+        action(send_beside, beside)
+
+        @pl.when((chip < z) & (z < chips - 1))
+        def _():
+            action(send_right, me + 2)
+
+        @pl.when((chip > z) & (z > 0))
+        def _():
+            action(send_left, me - 2)
+
+    def pass_on(chip, unit, with_facts):
+        origin = 2 * chip + core
+        move(origin, unit, send_beside, beside).wait_recv()
+        on(chip, lambda sems, target: move(origin, unit, sems, target).start())
+
+        @pl.when(with_facts)
+        def _():
+            move_facts(origin, send_beside, beside).wait_recv()
+            on(chip, lambda sems, target: move_facts(origin, sems, target).start())
+
+    def arrive(origin, unit):
+        move(origin, unit, send_beside, beside).wait_recv()
+
+    def arrive_facts(origin):
+        move_facts(origin, send_beside, beside).wait_recv()
+
+    max_ref[...] = jnp.full(max_ref.shape, masked_value, jnp.float32)
+    total_ref[...] = jnp.zeros(total_ref.shape, jnp.float32)
+    sum_ref[...] = jnp.zeros(sum_ref.shape, jnp.float32)
+
+    for g in range(groups):
+        for h in range(per_group):
+            columns = slice((g * per_group + h) * head_dim, (g * per_group + h + 1) * head_dim)
+            for row in range(2):
+                query_ref[row, g, h] = q_ref[row * block_len : (row + 1) * block_len, columns].T
+
+    def gain_row(origin, slot, g):
+        low = facts[origin, slot * groups : (slot + 1) * groups, :].astype(jnp.float32)
+        row = low[0:1, :]
+        for other in range(1, groups):
+            row = jnp.where(g == other, low[other : other + 1, :], row)
+        return row * rate
+
+    def scale_row(origin, slot, g):
+        base = 2 * groups + slot * groups
+        low = facts[origin, base : base + groups, :].astype(jnp.float32)
+        row = low[0:1, :]
+        for other in range(1, groups):
+            row = jnp.where(g == other, low[other : other + 1, :], row)
+        return row
+
+    def place_row(origin):
+        return facts[origin, 4 * groups : 4 * groups + 1, :].astype(jnp.float32)
+
+    def visit(parts, row, g, diagonal=False, blend=None):
+        turned = [(key, value.T, gain, scale) for key, value, gain, scale in parts]
+        if diagonal:
+            shape = (block_len, block_len)
+            visible = lax.broadcasted_iota(jnp.int32, shape, 0) <= lax.broadcasted_iota(
+                jnp.int32, shape, 1
+            )
+        if blend is not None:
+            is_low, low_share, high_share = blend
+
+        def held(ref, index):
+            if blend is None:
+                return ref[(row, g) + index]
+            return jnp.where(is_low, ref[(0, g) + index], ref[(1, g) + index])
+
+        def keep(ref, index, value):
+            if blend is None:
+                ref[(row, g) + index] = value
+            else:
+                ref[(0, g) + index] = jnp.where(is_low, value, ref[(0, g) + index])
+                ref[(1, g) + index] = jnp.where(is_low, ref[(1, g) + index], value)
+
+        def score(h):
+            if blend is None:
+                query = query_ref[row, g, h]
+            else:
+                query = query_ref[0, g, h] * low_share + query_ref[1, g, h] * high_share
+            result = [
+                jnp.dot(key, query, preferred_element_type=jnp.float32) for key, _, _, _ in turned
+            ]
+            if diagonal:
+                result[-1] = jnp.where(visible, result[-1], masked_value)
+            return result
+
+        def weigh(h, scores):
+            line = (slice(h, h + 1), slice(None))
+            old = held(max_ref, line)
+            top = old
+            for part, (_, _, gain, _) in zip(scores, turned):
+                top = jnp.maximum(top, jnp.max(part, axis=0, keepdims=True) * gain)
+            factor = jnp.exp2(old - top)
+            total = factor * held(total_ref, line)
+            rounded = []
+            for part, (_, _, gain, _) in zip(scores, turned):
+                weights = jnp.exp2(part * gain - top)
+                total = total + jnp.sum(weights, axis=0, keepdims=True)
+                rounded.append(weights.astype(jnp.bfloat16))
+            keep(max_ref, line, top)
+            keep(total_ref, line, total)
+            return rounded, factor
+
+        def gather(h, rounded, factor):
+            running = factor * held(sum_ref, (h,))
+            for part, (_, value, _, scale) in zip(rounded, turned):
+                running = running + scale * jnp.dot(
+                    value, part, preferred_element_type=jnp.float32
+                )
+            keep(sum_ref, (h,), running)
+
+        scores = score(0)
+        waiting = None
+        for h in range(per_group):
+            upcoming = score(h + 1) if h + 1 < per_group else None
+            if waiting is not None:
+                gather(h - 1, *waiting)
+            waiting = weigh(h, scores)
+            scores = upcoming
+        gather(per_group - 1, *waiting)
+
+    def part_of(origin, slot, g):
+        unit = slot * groups + g
+        return (
+            kv[origin, unit, :, :head_dim], kv[origin, unit, :, head_dim:],
+            gain_row(origin, slot, g), scale_row(origin, slot, g),
+        )
+
+    def visit_picked(origin, g):
+        is_low = place_row(origin) < place_row(me)
+        low_share = is_low.astype(jnp.float32)
+        high_share = 1.0 - low_share
+        low, high = part_of(origin, 0, g), part_of(origin, 1, g)
+        low_bits, high_bits = low_share.astype(jnp.bfloat16), high_share.astype(jnp.bfloat16)
+        narrow = (slice(None), slice(0, head_dim))
+        part = (
+            low[0] * low_bits[narrow] + high[0] * high_bits[narrow],
+            low[1] * low_bits[narrow] + high[1] * high_bits[narrow],
+            jnp.where(is_low, low[2], high[2]),
+            jnp.where(is_low, low[3], high[3]),
+        )
+        visit([part], None, g, blend=(is_low, low_bits, high_bits))
+
+    def pass_near(unit):
+        pass_on(first, unit, unit == 0)
+
+        @pl.when(middle == 1)
+        def _():
+            pass_on(second, unit, unit == 0)
+
+    @pl.loop(0, groups)
+    def _(g):
+        visit([part_of(me, 0, g)], 0, g, diagonal=True)
+        pass_near(g)
+
+    @pl.loop(0, groups)
+    def _(g):
+        visit([part_of(me, 1, g)], 1, g, diagonal=True)
+        pass_near(groups + g)
+
+    def attend_chip(chip):
+        def pair(g):
+            visit([part_of(2 * chip, 0, g), part_of(2 * chip + 1, 0, g)], 1, g)
+
+        return pair
+
+    @pl.loop(0, groups)
+    def _(g):
+        arrive(beside, g)
+
+        @pl.when(g == 0)
+        def _():
+            arrive_facts(beside)
+
+        attend_chip(z)(g)
+
+    @pl.loop(0, groups)
+    def _(g):
+        arrive(beside, groups + g)
+        visit_picked(beside, g)
+
+    @pl.loop(0, chips - 1)
+    def _(j):
+        chip = first * ((1 - j) * (2 - j) // 2) + second * (j * (2 - j)) + third * (j * (j - 1) // 2)
+        step = middle + j - 1
+        passing = second + (third - second) * step
+
+        @pl.loop(0, groups)
+        def _(g):
+            @pl.when((j >= 1) & (step <= 1))
+            def _():
+                pass_on(passing, g, g == 0)
+
+            arrive(2 * chip + 1 - core, g)
+
+            @pl.when(g == 0)
+            def _():
+                arrive_facts(2 * chip + 1 - core)
+
+            attend_chip(chip)(g)
+
+        @pl.loop(0, groups)
+        def _(g):
+            @pl.when((j >= 1) & (step <= 1))
+            def _():
+                pass_on(passing, groups + g, False)
+
+            visit_picked(2 * chip + core, g)
+            arrive(2 * chip + 1 - core, groups + g)
+            visit_picked(2 * chip + 1 - core, g)
+
+    @pl.loop(0, 2)
+    def _(row):
+        rows = pl.ds(pl.multiple_of(row * block_len, block_len), block_len)
+        for g in range(groups):
+            for h in range(per_group):
+                start = (g * per_group + h) * head_dim
+                mean = sum_ref[row, g, h] / total_ref[row, g, h : h + 1, :]
+                o_ref[rows, start : start + head_dim] = mean.astype(o_ref.dtype).T
+
+    def sent(origin, sems, target):
+        move_facts(origin, sems, target).wait_send()
+        for unit in range(units):
+            move(origin, unit, sems, target).wait_send()
+
+    @pl.when(z < chips - 1)
+    def _():
+        sent(me, send_right, me + 2)
+
+    @pl.when(z > 0)
+    def _():
+        sent(me, send_left, me - 2)
+
+    sent(me, send_beside, beside)
+
+    @pl.loop(0, chips)
+    def _(chip):
+        @pl.when(chip != z)
+        def _():
+            on(chip, lambda sems, target: sent(2 * chip + core, sems, target))
+
+
+def gather_attend(query, keys, values, k_scale, v_scale, block_place):
+    rows, head_count, head_dim = query.shape
+    groups = keys.shape[1]
+    slots = block_place.shape[0]
+    block_len = rows // slots
+    devices = lax.axis_size("ctx")
+    chips = devices // 2
+    units = slots * groups
+    per_group = head_count // groups
+    width = 2 * head_dim
+    own = jnp.concatenate([keys, values], axis=2).reshape(slots, block_len, groups, width)
+    own = own.transpose(0, 2, 1, 3).reshape(units, block_len, width)
+    listed = jnp.concatenate(
+        [k_scale.reshape(-1), v_scale.reshape(-1), block_place[:1].astype(jnp.bfloat16)]
+    )
+    listed = jnp.pad(listed, (0, 16 - listed.shape[0]))
+    own_facts = jnp.broadcast_to(listed[:, None], (16, width))
+    state = (2, groups, per_group)
+    tiles = 2 * devices + 1
+    pairs = tiles * block_len * block_len * head_count
+    whole = pl.BlockSpec(memory_space=pltpu.VMEM)
+    return pl.pallas_call(
+        functools.partial(
+            gather_attend_kernel, math.log2(math.e) / math.sqrt(head_dim), per_group, head_dim
+        ),
+        in_specs=[whole] * 3,
+        out_specs=whole,
+        scratch_shapes=[
+            pltpu.VMEM((devices, units, block_len, width), jnp.bfloat16),
+            pltpu.VMEM((devices, 16, width), jnp.bfloat16),
+            pltpu.VMEM(state + (head_dim, block_len), jnp.bfloat16),
+            pltpu.VMEM(state + (block_len,), jnp.float32),
+            pltpu.VMEM(state + (block_len,), jnp.float32),
+            pltpu.VMEM(state + (head_dim, block_len), jnp.float32),
+            pltpu.SemaphoreType.DMA((devices, units + 1)),
+            pltpu.SemaphoreType.DMA((chips, units + 1)),
+            pltpu.SemaphoreType.DMA((chips, units + 1)),
+            pltpu.SemaphoreType.DMA((chips, units + 1)),
+        ],
+        out_shape=jax.ShapeDtypeStruct((rows, head_count * head_dim), jnp.bfloat16),
+        compiler_params=pltpu.CompilerParams(
+            collective_id=1, has_side_effects=True, vmem_limit_bytes=40 * 1024 * 1024
+        ),
+        cost_estimate=pl.CostEstimate(
+            flops=4 * pairs * head_dim, bytes_accessed=8 << 20, transcendentals=pairs
+        ),
+    )(own, own_facts, query.reshape(rows, head_count * head_dim))
+
+
 def project_kernel(
     chunks,
     low_ref, high_ref, w_ref, o_ref,
@@ -257,9 +628,9 @@
         ).astype(jnp.bfloat16)
 
 
-def project(low, high, weight):
+def project(attended, weight):
     depth, columns = weight.shape
-    rows = 2 * low.shape[0]
+    rows = attended.shape[0]
     part = rows // 4
     step = COLUMN_STEP
     chunks = columns // step
@@ -271,7 +642,7 @@
             grid=(chunks + 2 * LAG,),
             in_specs=[
                 pl.BlockSpec((rows // 2, depth), lambda t: (0, 0)),
-                pl.BlockSpec((rows // 2, depth), lambda t: (0, 0)),
+                pl.BlockSpec((rows // 2, depth), lambda t: (1, 0)),
                 pl.BlockSpec((depth, step), lambda t: (0, jnp.minimum(t, last))),
             ],
             out_specs=pl.BlockSpec((part, step), lambda t: (0, jnp.maximum(t - 2 * LAG, 0))),
@@ -296,7 +667,7 @@
             flops=2 * rows * depth * columns, bytes_accessed=2 * depth * columns,
             transcendentals=0,
         ),
-    )(low, high, weight)
+    )(attended, attended, weight)
 
 
 def body(query, keys, values, k_scale, v_scale, block_place, out_weight):
@@ -306,6 +677,9 @@
     devices = lax.axis_size("ctx")
     blocks = slots * devices
     block_len = rows // slots
+    if lax.axis_size("head") == 4 and devices == 8 and slots == 2 and block_len == 2 * head_dim:
+        mixed_heads = gather_attend(query, keys, values, k_scale, v_scale, block_place)
+        return project(mixed_heads, out_weight)
     width = group_count * head_dim
     facts = jnp.concatenate(
         [k_scale, v_scale, block_place[:, None].astype(jnp.bfloat16)], axis=1
@@ -334,8 +708,6 @@
     state = attend(known, flat, low_part, group_count, head_dim, 1)
     low = attend(known, flat, low_part, group_count, head_dim, 0)
     high = attend(known, flat, high_part, group_count, head_dim, 1, state)
-    if lax.axis_size("head") == 4:
-        return project(low, high, out_weight)
     term = jnp.dot(jnp.concatenate([low, high]), out_weight, preferred_element_type=jnp.float32)
     return lax.psum_scatter(
         term.astype(jnp.bfloat16), "head", scatter_dimension=0, tiled=True

time: 176 us -> 143 us (0.81); the launches traced: 174 us -> 143 us
  waiting for transfers between devices: 29.4 us -> 0 us
  Pallas kernels: 110 us -> 134 us
  between operations: 13.5 us -> 0.05 us
  local copies, waits for them, and re-layouts: 17 us -> 6.73 us
    all_gather x2 -> x0, waiting for transfers between devices: 29.4 us -> none  [the longest x1 29.4 us: body(): lax.all_gather(jnp.concatenate(payload(0) + [facts]), 'ctx', axis=0)]
    pallas_call x3 -> x1, Pallas kernels: 33.6 us -> 56.4 us  [gather_attend(): pl.pallas_call(functools.partial(gather_attend_kernel, math.log2(math.e)...]
    unnamed x18 -> x6, local copies, waits for them, and re-layouts: 13.3 us -> 4.96 us
    slice x3 -> x0, local copies, waits for them, and re-layouts: 3.02 us -> none  [the longest x1 1.15 us: payload(): key = keys[part].reshape(block_len, width)]
  transfers between devices with their start and end apart: 2 -> 0, of which waited for: 1 -> 0; matrix products, arithmetic and copies ran while one was open for 3% -> 0% of each run, Pallas kernels for 17% -> 0%
where the time goes in v1:
time: 143 us
  Pallas kernels  134 us (94%)
  local copies, waits for them, and re-layouts  6.73 us (5%)
  other arithmetic  2.36 us (2%)
    pallas_call x1, Pallas kernels, project(): pl.pallas_call(functools.partial(project_kernel, chunks), grid_spec=pltpu...  77.2 us
    pallas_call x1, Pallas kernels, gather_attend(): pl.pallas_call(functools.partial(gather_attend_kernel, math.log2(math.e)...  56.4 us
    unnamed x6, local copies, waits for them, and re-layouts  4.96 us

profile of v1, /device:TPU:0, one launch (start us, length us, event | category | flops | bytes accessed | tf_op | source)
XLA Modules:
  0.0 142.6 jit_solution(5406465621276740636)
XLA Ops:
  0.0 0.0 copy-start.1
  0.0 0.9 reshape.18
  0.9 0.7 reshape.19
  1.6 0.7 convert.3
  2.3 0.1 select_maximum_fusion
  2.4 0.1 broadcast_in_dim.2.own_facts
  2.5 1.6 %pad_maximum_fusion = bf16[512,2,256]{2,1,0:T(2,128)(2,1)S(1)} fusion(bf16[512,2,128]{2,1,0:T(2,128)(2,1)} %param.9, bf16[512,2,128]{2,1,0:T(2,128)(2,1)} %param.8), kind=kLoop, calls=%fused_computation.1 | loop fusion | flops 1048576 | bytes 1048576 | tf_op jit(solution)/shard_map/concatenate | solution.py:513
  4.1 0.1 copy.8
  4.1 0.0 copy-done.1
  4.2 0.5 copy.11
  4.7 56.4 %shard_map.73.low_ref.high_ref = bf16[512,2048]{1,0:T(8,128)(2,1)S(1)} custom-call(bf16[4,256,256]{2,1,0:T(8,128)(2,1)S(1)} %bitcast.10, bf16[16,256]{1,0:T(8,128)(2,1)S(1)} %broadcast_in_dim.2.own_facts, bf16[512,2048]{1,0:T(8,128)(2,1)S(1)} %bitcast.9), custom_call_target="tpu_custom_call" | custom-call | flops 9126805504 | bytes 8388608 | tf_op jit(solution)/shard_map/pallas_call | solution.py:524
  61.1 0.0 copy-start
  61.1 1.3 copy-done
  62.4 77.2 %shard_map.74 = bf16[128,8192]{1,0:T(8,128)(2,1)} custom-call(bf16[512,2048]{1,0:T(8,128)(2,1)} %copy-done, bf16[512,2048]{1,0:T(8,128)(2,1)} %copy-done, bf16[2048,8192]{1,0:T(8,128)(2,1)} %w_ref.1), custom_call_target="tpu_custom_call" | custom-call | flops 17179869184 | bytes 33554432 | tf_op jit(solution)/shard_map/pallas_call | solution.py:638
  139.5 3.1 %copy.13 = bf16[128,8192]{1,0:T(8,128)(2,1)} copy(bf16[128,8192]{1,0:T(8,128)(2,1)} %shard_map.74) | data formatting | bytes 4194304
Async XLA Ops:
  0.0 4.1 %copy-start.1 = (bf16[512,16,128]{2,1,0:T(8,128)(2,1)S(1)}, bf16[512,16,128]{2,1,0:T(8,128)(2,1)}, u32[]{:S(2)}) copy-start(bf16[512,16,128]{2,1,0:T(8,128)(2,1)} %param.7) | copy-start | bytes 6291460
  61.1 1.3 copy-start

commit v2 on v1

--- a/solution.py
+++ b/solution.py
@@ -178,11 +178,13 @@
     return results if len(results) > 1 else results[0]
 
 
-def gather_attend_kernel(
-    rate, per_group, head_dim,
-    own_ref, own_facts, q_ref, o_ref,
+def mix_kernel(
+    rate, per_group, head_dim, chunks,
+    block_place, own_ref, own_k_scale, own_v_scale, q_ref, w_ref, o_ref,
     kv, facts, query_ref, max_ref, total_ref, sum_ref,
+    attended, held_w, terms, arrived, passed, ended,
     recv, send_right, send_left, send_beside,
+    load_w, send_one, recv_one, send_two, recv_two,
 ):
     groups = kv.shape[1] // 2
     units = kv.shape[1]
@@ -197,6 +199,21 @@
     second = 2 - half
     third = 3 * (1 - half)
 
+    head = lax.axis_index("head")
+    along_x = head + 1 - 2 * (head % 2)
+    along_y = (head + 2) % 4
+    step_columns = held_w.shape[2]
+    part = o_ref.shape[0]
+
+    def fetch(chunk):
+        columns = pl.ds(pl.multiple_of(chunk * step_columns, step_columns), step_columns)
+        return pltpu.make_async_copy(
+            w_ref.at[:, columns], held_w.at[chunk % 3], load_w.at[chunk % 3]
+        )
+
+    fetch(0).start()
+    fetch(1).start()
+
     barrier = pltpu.get_barrier_semaphore()
 
     def greet(device):
@@ -204,6 +221,10 @@
             barrier, inc=1, device_id={"ctx": device}, device_id_type=pl.DeviceIdType.MESH
         )
 
+    for partner in (along_x, along_y):
+        pl.semaphore_signal(
+            barrier, inc=1, device_id={"head": partner}, device_id_type=pl.DeviceIdType.MESH
+        )
     greet(beside)
 
     @pl.when(z > 0)
@@ -216,15 +237,24 @@
 
     for unit in range(units):
         kv[me, unit] = own_ref[unit]
-    facts[me] = own_facts[...]
+    shape = (1, facts.shape[2])
+    for slot in range(2):
+        for g in range(groups):
+            unit = slot * groups + g
+            for base, ref in ((0, own_k_scale), (2 * groups, own_v_scale)):
+                one = ref[slot : slot + 1, g : g + 1].astype(jnp.float32)
+                facts[me, base + unit : base + unit + 1, :] = jnp.broadcast_to(one, shape)
+    facts[me, 4 * groups : 4 * groups + 1, :] = jnp.full(
+        shape, block_place[0].astype(jnp.float32)
+    )
 
     @pl.when((z > 0) & (z < chips - 1))
     def _():
-        pl.semaphore_wait(barrier, 3)
+        pl.semaphore_wait(barrier, 5)
 
     @pl.when((z == 0) | (z == chips - 1))
     def _():
-        pl.semaphore_wait(barrier, 2)
+        pl.semaphore_wait(barrier, 4)
 
     def move(origin, unit, sems, target):
         return pltpu.make_async_remote_copy(
@@ -320,64 +350,80 @@
         if blend is not None:
             is_low, low_share, high_share = blend
 
+        cut = block_len // 2
+
         def held(ref, index):
             if blend is None:
                 return ref[(row, g) + index]
-            return jnp.where(is_low, ref[(0, g) + index], ref[(1, g) + index])
+            return jnp.where(is_low[:, :cut], ref[(0, g) + index], ref[(1, g) + index])
 
         def keep(ref, index, value):
             if blend is None:
                 ref[(row, g) + index] = value
             else:
-                ref[(0, g) + index] = jnp.where(is_low, value, ref[(0, g) + index])
-                ref[(1, g) + index] = jnp.where(is_low, ref[(1, g) + index], value)
-
-        def score(h):
+                share = is_low[:, :cut]
+                ref[(0, g) + index] = jnp.where(share, value, ref[(0, g) + index])
+                ref[(1, g) + index] = jnp.where(share, ref[(1, g) + index], value)
+
+        steps = [(h, slice(n * cut, (n + 1) * cut)) for h in range(per_group) for n in range(block_len // cut)]
+
+        def score(step):
+            h, columns = steps[step]
+            at = (h, slice(None), columns)
             if blend is None:
-                query = query_ref[row, g, h]
+                query = query_ref[(row, g) + at]
             else:
-                query = query_ref[0, g, h] * low_share + query_ref[1, g, h] * high_share
+                query = (
+                    query_ref[(0, g) + at] * low_share[:, :cut]
+                    + query_ref[(1, g) + at] * high_share[:, :cut]
+                )
             result = [
                 jnp.dot(key, query, preferred_element_type=jnp.float32) for key, _, _, _ in turned
             ]
             if diagonal:
-                result[-1] = jnp.where(visible, result[-1], masked_value)
+                result[-1] = jnp.where(visible[:, columns], result[-1], masked_value)
             return result
 
-        def weigh(h, scores):
-            line = (slice(h, h + 1), slice(None))
+        def weigh(step, scores):
+            h, columns = steps[step]
+            line = (slice(h, h + 1), columns)
             old = held(max_ref, line)
             top = old
             for part, (_, _, gain, _) in zip(scores, turned):
-                top = jnp.maximum(top, jnp.max(part, axis=0, keepdims=True) * gain)
+                top = jnp.maximum(top, jnp.max(part, axis=0, keepdims=True) * gain[:, :cut])
             factor = jnp.exp2(old - top)
             total = factor * held(total_ref, line)
             rounded = []
             for part, (_, _, gain, _) in zip(scores, turned):
-                weights = jnp.exp2(part * gain - top)
+                weights = jnp.exp2(part * gain[:, :cut] - top)
                 total = total + jnp.sum(weights, axis=0, keepdims=True)
                 rounded.append(weights.astype(jnp.bfloat16))
             keep(max_ref, line, top)
             keep(total_ref, line, total)
             return rounded, factor
 
-        def gather(h, rounded, factor):
-            running = factor * held(sum_ref, (h,))
+        def gather(step, rounded, factor):
+            h, columns = steps[step]
+            at = (h, slice(None), columns)
+            running = factor * held(sum_ref, at)
             for part, (_, value, _, scale) in zip(rounded, turned):
-                running = running + scale * jnp.dot(
+                running = running + scale[:, :cut] * jnp.dot(
                     value, part, preferred_element_type=jnp.float32
                 )
-            keep(sum_ref, (h,), running)
-
-        scores = score(0)
-        waiting = None
-        for h in range(per_group):
-            upcoming = score(h + 1) if h + 1 < per_group else None
-            if waiting is not None:
-                gather(h - 1, *waiting)
-            waiting = weigh(h, scores)
-            scores = upcoming
-        gather(per_group - 1, *waiting)
+            keep(sum_ref, at, running)
+
+        depth, lag = 2, 1
+        scores = {}
+        waiting = {}
+        for step in range(depth):
+            scores[step] = score(step)
+        for step in range(len(steps) + lag):
+            if step + depth < len(steps):
+                scores[step + depth] = score(step + depth)
+            if step >= lag:
+                gather(step - lag, *waiting.pop(step - lag))
+            if step < len(steps):
+                waiting[step] = weigh(step, scores.pop(step))
 
     def part_of(origin, slot, g):
         unit = slot * groups + g
@@ -411,12 +457,10 @@
     @pl.loop(0, groups)
     def _(g):
         visit([part_of(me, 0, g)], 0, g, diagonal=True)
-        pass_near(g)
 
     @pl.loop(0, groups)
     def _(g):
         visit([part_of(me, 1, g)], 1, g, diagonal=True)
-        pass_near(groups + g)
 
     def attend_chip(chip):
         def pair(g):
@@ -438,6 +482,9 @@
     def _(g):
         arrive(beside, groups + g)
         visit_picked(beside, g)
+
+    for unit in range(units):
+        pass_near(unit)
 
     @pl.loop(0, chips - 1)
     def _(j):
@@ -476,7 +523,62 @@
             for h in range(per_group):
                 start = (g * per_group + h) * head_dim
                 mean = sum_ref[row, g, h] / total_ref[row, g, h : h + 1, :]
-                o_ref[rows, start : start + head_dim] = mean.astype(o_ref.dtype).T
+                attended[rows, start : start + head_dim] = mean.astype(attended.dtype).T
+
+    def first_copy(c):
+        near = along_x + (c % 2) * (along_y - along_x)
+        return pltpu.make_async_remote_copy(
+            src_ref=terms.at[c, pl.ds(0, 2)], dst_ref=arrived.at[c],
+            send_sem=send_one.at[c], recv_sem=recv_one.at[c],
+            device_id={"head": near}, device_id_type=pl.DeviceIdType.MESH,
+        )
+
+    def second_copy(c):
+        far = along_y + (c % 2) * (along_x - along_y)
+        return pltpu.make_async_remote_copy(
+            src_ref=passed.at[c], dst_ref=ended.at[c],
+            send_sem=send_two.at[c], recv_sem=recv_two.at[c],
+            device_id={"head": far}, device_id_type=pl.DeviceIdType.MESH,
+        )
+
+    @pl.loop(0, chunks + 2 * LAG)
+    def _(t):
+        @pl.when(t < chunks)
+        def _():
+            @pl.when(t + 2 < chunks)
+            def _():
+                fetch(t + 2).start()
+
+            fetch(t).wait()
+            term = jnp.dot(
+                attended[...], held_w[t % 3], preferred_element_type=jnp.float32
+            ).astype(jnp.bfloat16)
+            for owner in range(4):
+                over_x = (head + owner) % 2
+                over_y = (head // 2 + owner // 2) % 2
+                place = 3 - over_x - over_y - over_x + (t % 2) * (over_x - over_y)
+                terms[t, place] = term[owner * part : (owner + 1) * part]
+            first_copy(t).start()
+
+        @pl.when((t >= LAG) & (t < chunks + LAG))
+        def _():
+            c = t - LAG
+            first_copy(c).wait()
+            passed[c] = (
+                arrived[c, 0].astype(jnp.float32) + terms[c, 2].astype(jnp.float32)
+            ).astype(jnp.bfloat16)
+            second_copy(c).start()
+
+        @pl.when(t >= 2 * LAG)
+        def _():
+            c = t - 2 * LAG
+            second_copy(c).wait()
+            columns = pl.ds(pl.multiple_of(c * step_columns, step_columns), step_columns)
+            o_ref[:, columns] = (
+                arrived[c, 1].astype(jnp.float32)
+                + terms[c, 3].astype(jnp.float32)
+                + ended[c].astype(jnp.float32)
+            ).astype(jnp.bfloat16)
 
     def sent(origin, sems, target):
         move_facts(origin, sems, target).wait_send()
@@ -500,8 +602,9 @@
             on(chip, lambda sems, target: sent(2 * chip + core, sems, target))
 
 
-def gather_attend(query, keys, values, k_scale, v_scale, block_place):
+def mix(query, keys, values, k_scale, v_scale, block_place, weight):
     rows, head_count, head_dim = query.shape
+    depth, columns = weight.shape
     groups = keys.shape[1]
     slots = block_place.shape[0]
     block_len = rows // slots
@@ -510,164 +613,57 @@
     units = slots * groups
     per_group = head_count // groups
     width = 2 * head_dim
+    part = rows // lax.axis_size("head")
+    step = COLUMN_STEP
+    chunks = columns // step
     own = jnp.concatenate([keys, values], axis=2).reshape(slots, block_len, groups, width)
     own = own.transpose(0, 2, 1, 3).reshape(units, block_len, width)
-    listed = jnp.concatenate(
-        [k_scale.reshape(-1), v_scale.reshape(-1), block_place[:1].astype(jnp.bfloat16)]
-    )
-    listed = jnp.pad(listed, (0, 16 - listed.shape[0]))
-    own_facts = jnp.broadcast_to(listed[:, None], (16, width))
     state = (2, groups, per_group)
-    tiles = 2 * devices + 1
-    pairs = tiles * block_len * block_len * head_count
+    pairs = (2 * devices + 1) * block_len * block_len * head_count
     whole = pl.BlockSpec(memory_space=pltpu.VMEM)
     return pl.pallas_call(
         functools.partial(
-            gather_attend_kernel, math.log2(math.e) / math.sqrt(head_dim), per_group, head_dim
+            mix_kernel, math.log2(math.e) / math.sqrt(head_dim), per_group, head_dim, chunks
         ),
-        in_specs=[whole] * 3,
+        in_specs=[pl.BlockSpec(memory_space=pltpu.SMEM)]
+        + [whole] * 4
+        + [pl.BlockSpec(memory_space=pl.ANY)],
         out_specs=whole,
         scratch_shapes=[
             pltpu.VMEM((devices, units, block_len, width), jnp.bfloat16),
-            pltpu.VMEM((devices, 16, width), jnp.bfloat16),
+            pltpu.VMEM((devices, 16, width), jnp.float32),
             pltpu.VMEM(state + (head_dim, block_len), jnp.bfloat16),
             pltpu.VMEM(state + (block_len,), jnp.float32),
             pltpu.VMEM(state + (block_len,), jnp.float32),
             pltpu.VMEM(state + (head_dim, block_len), jnp.float32),
+            pltpu.VMEM((rows, depth), jnp.bfloat16),
+            pltpu.VMEM((3, depth, step), jnp.bfloat16),
+            pltpu.VMEM((chunks, 4, part, step), jnp.bfloat16),
+            pltpu.VMEM((chunks, 2, part, step), jnp.bfloat16),
+            pltpu.VMEM((chunks, part, step), jnp.bfloat16),
+            pltpu.VMEM((chunks, part, step), jnp.bfloat16),
             pltpu.SemaphoreType.DMA((devices, units + 1)),
             pltpu.SemaphoreType.DMA((chips, units + 1)),
             pltpu.SemaphoreType.DMA((chips, units + 1)),
             pltpu.SemaphoreType.DMA((chips, units + 1)),
+            pltpu.SemaphoreType.DMA((3,)),
+            pltpu.SemaphoreType.DMA((chunks,)),
+            pltpu.SemaphoreType.DMA((chunks,)),
+            pltpu.SemaphoreType.DMA((chunks,)),
+            pltpu.SemaphoreType.DMA((chunks,)),
         ],
-        out_shape=jax.ShapeDtypeStruct((rows, head_count * head_dim), jnp.bfloat16),
+        out_shape=jax.ShapeDtypeStruct((part, columns), jnp.bfloat16),
         compiler_params=pltpu.CompilerParams(
-            collective_id=1, has_side_effects=True, vmem_limit_bytes=40 * 1024 * 1024
+            collective_id=0, has_side_effects=True, vmem_limit_bytes=47 * 1024 * 1024
         ),
         cost_estimate=pl.CostEstimate(
-            flops=4 * pairs * head_dim, bytes_accessed=8 << 20, transcendentals=pairs
+            flops=4 * pairs * head_dim + 2 * rows * depth * columns,
+            bytes_accessed=2 * depth * columns, transcendentals=pairs,
         ),
-    )(own, own_facts, query.reshape(rows, head_count * head_dim))
-
-
-def project_kernel(
-    chunks,
-    low_ref, high_ref, w_ref, o_ref,
-    lhs, sent, kept, arrived, passed, ended,
-    send_one, recv_one, send_two, recv_two,
-):
-    t = pl.program_id(0)
-    me = lax.axis_index("head")
-    along_x = me + 1 - 2 * (me % 2)
-    along_y = (me + 2) % 4
-    part = low_ref.shape[0] // 2
-
-    @pl.when(t == 0)
-    def _():
-        barrier = pltpu.get_barrier_semaphore()
-        for partner in (along_x, along_y):
-            pl.semaphore_signal(
-                barrier, inc=1, device_id={"head": partner},
-                device_id_type=pl.DeviceIdType.MESH,
-            )
-        for parity in range(2):
-            near, far = (along_x, along_y) if parity == 0 else (along_y, along_x)
-            for slot, owner in enumerate((3 - me, near, far, me)):
-                rows = pl.ds(pl.multiple_of((owner % 2) * part, part), part)
-
-                @pl.when(owner // 2 == 0)
-                def _():
-                    lhs[parity, slot * part : (slot + 1) * part, :] = low_ref[rows, :]
-
-                @pl.when(owner // 2 == 1)
-                def _():
-                    lhs[parity, slot * part : (slot + 1) * part, :] = high_ref[rows, :]
-
-        pl.semaphore_wait(barrier, 2)
-
-    def first_copy(c):
-        near = along_x + (c % 2) * (along_y - along_x)
-        return pltpu.make_async_remote_copy(
-            src_ref=sent.at[c], dst_ref=arrived.at[c],
-            send_sem=send_one.at[c], recv_sem=recv_one.at[c],
-            device_id={"head": near}, device_id_type=pl.DeviceIdType.MESH,
-        )
-
-    def second_copy(c):
-        far = along_y + (c % 2) * (along_x - along_y)
-        return pltpu.make_async_remote_copy(
-            src_ref=passed.at[c], dst_ref=ended.at[c],
-            send_sem=send_two.at[c], recv_sem=recv_two.at[c],
-            device_id={"head": far}, device_id_type=pl.DeviceIdType.MESH,
-        )
-
-    @pl.when(t < chunks)
-    def _():
-        term = jnp.dot(lhs[t % 2], w_ref[...], preferred_element_type=jnp.float32)
-        term = term.astype(jnp.bfloat16)
-        sent[t] = term[: 2 * part]
-        kept[t] = term[2 * part :]
-        first_copy(t).start()
-
-    @pl.when((t >= LAG) & (t < chunks + LAG))
-    def _():
-        c = t - LAG
-        first_copy(c).wait()
-        passed[c] = (
-            arrived[c, :part, :].astype(jnp.float32) + kept[c, :part, :].astype(jnp.float32)
-        ).astype(jnp.bfloat16)
-        second_copy(c).start()
-
-    @pl.when(t >= 2 * LAG)
-    def _():
-        c = t - 2 * LAG
-        second_copy(c).wait()
-        o_ref[...] = (
-            arrived[c, part:, :].astype(jnp.float32)
-            + kept[c, part:, :].astype(jnp.float32)
-            + ended[c].astype(jnp.float32)
-        ).astype(jnp.bfloat16)
-
-
-def project(attended, weight):
-    depth, columns = weight.shape
-    rows = attended.shape[0]
-    part = rows // 4
-    step = COLUMN_STEP
-    chunks = columns // step
-    last = chunks - 1
-    return pl.pallas_call(
-        functools.partial(project_kernel, chunks),
-        grid_spec=pltpu.PrefetchScalarGridSpec(
-            num_scalar_prefetch=0,
-            grid=(chunks + 2 * LAG,),
-            in_specs=[
-                pl.BlockSpec((rows // 2, depth), lambda t: (0, 0)),
-                pl.BlockSpec((rows // 2, depth), lambda t: (1, 0)),
-                pl.BlockSpec((depth, step), lambda t: (0, jnp.minimum(t, last))),
-            ],
-            out_specs=pl.BlockSpec((part, step), lambda t: (0, jnp.maximum(t - 2 * LAG, 0))),
-            scratch_shapes=[
-                pltpu.VMEM((2, rows, depth), jnp.bfloat16),
-                pltpu.VMEM((chunks, 2 * part, step), jnp.bfloat16),
-                pltpu.VMEM((chunks, 2 * part, step), jnp.bfloat16),
-                pltpu.VMEM((chunks, 2 * part, step), jnp.bfloat16),
-                pltpu.VMEM((chunks, part, step), jnp.bfloat16),
-                pltpu.VMEM((chunks, part, step), jnp.bfloat16),
-                pltpu.SemaphoreType.DMA((chunks,)),
-                pltpu.SemaphoreType.DMA((chunks,)),
-                pltpu.SemaphoreType.DMA((chunks,)),
-                pltpu.SemaphoreType.DMA((chunks,)),
-            ],
-        ),
-        out_shape=jax.ShapeDtypeStruct((part, columns), jnp.bfloat16),
-        compiler_params=pltpu.CompilerParams(
-            collective_id=0, has_side_effects=True, vmem_limit_bytes=56 * 1024 * 1024
-        ),
-        cost_estimate=pl.CostEstimate(
-            flops=2 * rows * depth * columns, bytes_accessed=2 * depth * columns,
-            transcendentals=0,
-        ),
-    )(attended, attended, weight)
+    )(
+        block_place, own, k_scale, v_scale,
+        query.reshape(rows, head_count * head_dim), weight,
+    )
 
 
 def body(query, keys, values, k_scale, v_scale, block_place, out_weight):
@@ -678,8 +674,7 @@
     blocks = slots * devices
     block_len = rows // slots
     if lax.axis_size("head") == 4 and devices == 8 and slots == 2 and block_len == 2 * head_dim:
-        mixed_heads = gather_attend(query, keys, values, k_scale, v_scale, block_place)
-        return project(mixed_heads, out_weight)
+        return mix(query, keys, values, k_scale, v_scale, block_place, out_weight)
     width = group_count * head_dim
     facts = jnp.concatenate(
         [k_scale, v_scale, block_place[:, None].astype(jnp.bfloat16)], axis=1

time: 143 us -> 125 us (0.87)
  Pallas kernels: 134 us -> 121 us
  local copies, waits for them, and re-layouts: 6.73 us -> 2.06 us
    pallas_call x2 -> x1, Pallas kernels: 134 us -> 121 us  [mix(): pl.pallas_call(functools.partial(mix_kernel, math.log2(math.e) / math.sqr...]
    unnamed x6 -> x10, local copies, waits for them, and re-layouts: 4.96 us -> 1.98 us
    reshape x3 -> x1, local copies, waits for them, and re-layouts: 1.7 us -> 0.07 us  [mix(): jnp.concatenate([keys, values], axis=2)]
where the time goes in v2:
time: 125 us
  Pallas kernels  121 us (97%)
  local copies, waits for them, and re-layouts  2.06 us (2%)
  other arithmetic  1.73 us (1%)
    pallas_call x1, Pallas kernels, mix(): pl.pallas_call(functools.partial(mix_kernel, math.log2(math.e) / math.sqr...  121 us

profile of v2, /device:TPU:0, one launch (start us, length us, event | category | flops | bytes accessed | tf_op | source)
XLA Modules:
  0.0 125.3 jit_solution(10786395900200604136)
XLA Ops:
  0.0 0.0 copy-start.3
  0.0 1.7 %pad_maximum_fusion = bf16[512,2,256]{2,1,0:T(2,128)(2,1)S(1)} fusion(bf16[512,2,128]{2,1,0:T(2,128)(2,1)} %param.9, bf16[512,2,128]{2,1,0:T(2,128)(2,1)} %param.8), kind=kLoop, calls=%fused_computation.1 | loop fusion | flops 1048576 | bytes 1048576 | tf_op jit(solution)/shard_map/concatenate | solution.py:619
  1.7 0.1 copy.8
  1.8 0.0 copy-done.3
  1.8 0.0 copy-start
  1.8 0.0 copy-start.1
  1.9 0.0 copy-start.2
  1.9 0.5 copy.11
  2.4 0.1 copy-done
  2.5 0.0 copy-done.1
  2.5 0.0 copy-done.2
  2.5 121.4 %shard_map.73 = bf16[128,8192]{1,0:T(8,128)(2,1)S(1)} custom-call(s32[2]{0:T(128)S(1)} %copy-done, bf16[4,256,256]{2,1,0:T(8,128)(2,1)S(1)} %bitcast.9, bf16[2,2]{1,0:T(2,128)(2,1)S(1)} %copy-done.1, bf16[2,2]{1,0:T(2,128)(2,1)S(1)} %copy-done.2, bf16[512,2048]{1,0:T(8,128)(2,1)S(1)} %bitcast.8, bf16[2048,8192]{1,0:T(8,128)(2,1)} %w_ref.1), custom_call_target="tpu_custom_call" | custom-call | flops 26306674688 | bytes 33554432 | tf_op jit(solution)/shard_map/pallas_call | solution.py:624
  124.0 1.3 %copy.13 = bf16[128,8192]{1,0:T(8,128)(2,1)} copy(bf16[128,8192]{1,0:T(8,128)(2,1)S(1)} %shard_map.73) | data formatting | bytes 4194304
Async XLA Ops:
  0.0 1.8 %copy-start.3 = (bf16[512,16,128]{2,1,0:T(8,128)(2,1)S(1)}, bf16[512,16,128]{2,1,0:T(8,128)(2,1)}, u32[]{:S(2)}) copy-start(bf16[512,16,128]{2,1,0:T(8,128)(2,1)} %param.7) | copy-start | bytes 6291460
  1.8 0.7 copy-start
  1.8 0.7 copy-start.1
  1.9 0.7 copy-start.2

commit v3 on v2

--- a/solution.py
+++ b/solution.py
@@ -9,8 +9,8 @@
 from jax.sharding import PartitionSpec as P
 
 masked_value = -1e30
-COLUMN_STEP = 512
-LAG = 3
+COLUMN_STEP = 256
+LAG = 6
 
 
 def attend_kernel(
@@ -238,15 +238,16 @@
     for unit in range(units):
         kv[me, unit] = own_ref[unit]
     shape = (1, facts.shape[2])
-    for slot in range(2):
-        for g in range(groups):
-            unit = slot * groups + g
-            for base, ref in ((0, own_k_scale), (2 * groups, own_v_scale)):
-                one = ref[slot : slot + 1, g : g + 1].astype(jnp.float32)
-                facts[me, base + unit : base + unit + 1, :] = jnp.broadcast_to(one, shape)
-    facts[me, 4 * groups : 4 * groups + 1, :] = jnp.full(
-        shape, block_place[0].astype(jnp.float32)
-    )
+    listed = [
+        jnp.broadcast_to(ref[slot : slot + 1, g : g + 1].astype(jnp.float32), shape)
+        for ref in (own_k_scale, own_v_scale)
+        for slot in range(2)
+        for g in range(groups)
+    ]
+    listed.append(jnp.full(shape, block_place[0].astype(jnp.float32)))
+    spare = facts.shape[1] - len(listed)
+    listed.append(jnp.zeros((spare,) + shape[1:], jnp.float32))
+    facts[me] = jnp.concatenate(listed, axis=0).astype(facts.dtype)
 
     @pl.when((z > 0) & (z < chips - 1))
     def _():
@@ -270,20 +271,24 @@
             device_id={"ctx": target}, device_id_type=pl.DeviceIdType.MESH,
         )
 
-    def send_own(sems, target):
-        move_facts(me, sems, target).start()
-        for unit in range(units):
-            move(me, unit, sems, target).start()
-
-    @pl.when(z < chips - 1)
-    def _():
-        send_own(send_right, me + 2)
-
-    @pl.when(z > 0)
-    def _():
-        send_own(send_left, me - 2)
-
-    send_own(send_beside, beside)
+    def send_own(slot):
+        def start(sems, target):
+            if slot == 0:
+                move_facts(me, sems, target).start()
+            for unit in range(slot * groups, (slot + 1) * groups):
+                move(me, unit, sems, target).start()
+
+        @pl.when(z < chips - 1)
+        def _():
+            start(send_right, me + 2)
+
+        @pl.when(z > 0)
+        def _():
+            start(send_left, me - 2)
+
+        start(send_beside, beside)
+
+    send_own(0)
 
     def on(chip, action):
         action(send_beside, beside)
@@ -350,18 +355,18 @@
         if blend is not None:
             is_low, low_share, high_share = blend
 
-        cut = block_len // 2
+        cut = facts.shape[2]
 
         def held(ref, index):
             if blend is None:
                 return ref[(row, g) + index]
-            return jnp.where(is_low[:, :cut], ref[(0, g) + index], ref[(1, g) + index])
+            return jnp.where(is_low, ref[(0, g) + index], ref[(1, g) + index])
 
         def keep(ref, index, value):
             if blend is None:
                 ref[(row, g) + index] = value
             else:
-                share = is_low[:, :cut]
+                share = is_low
                 ref[(0, g) + index] = jnp.where(share, value, ref[(0, g) + index])
                 ref[(1, g) + index] = jnp.where(share, ref[(1, g) + index], value)
 
@@ -374,8 +379,8 @@
                 query = query_ref[(row, g) + at]
             else:
                 query = (
-                    query_ref[(0, g) + at] * low_share[:, :cut]
-                    + query_ref[(1, g) + at] * high_share[:, :cut]
+                    query_ref[(0, g) + at] * low_share
+                    + query_ref[(1, g) + at] * high_share
                 )
             result = [
                 jnp.dot(key, query, preferred_element_type=jnp.float32) for key, _, _, _ in turned
@@ -390,12 +395,12 @@
             old = held(max_ref, line)
             top = old
             for part, (_, _, gain, _) in zip(scores, turned):
-                top = jnp.maximum(top, jnp.max(part, axis=0, keepdims=True) * gain[:, :cut])
+                top = jnp.maximum(top, jnp.max(part, axis=0, keepdims=True) * gain)
             factor = jnp.exp2(old - top)
             total = factor * held(total_ref, line)
             rounded = []
             for part, (_, _, gain, _) in zip(scores, turned):
-                weights = jnp.exp2(part * gain[:, :cut] - top)
+                weights = jnp.exp2(part * gain - top)
                 total = total + jnp.sum(weights, axis=0, keepdims=True)
                 rounded.append(weights.astype(jnp.bfloat16))
             keep(max_ref, line, top)
@@ -407,7 +412,7 @@
             at = (h, slice(None), columns)
             running = factor * held(sum_ref, at)
             for part, (_, value, _, scale) in zip(rounded, turned):
-                running = running + scale[:, :cut] * jnp.dot(
+                running = running + scale * jnp.dot(
                     value, part, preferred_element_type=jnp.float32
                 )
             keep(sum_ref, at, running)
@@ -438,10 +443,9 @@
         high_share = 1.0 - low_share
         low, high = part_of(origin, 0, g), part_of(origin, 1, g)
         low_bits, high_bits = low_share.astype(jnp.bfloat16), high_share.astype(jnp.bfloat16)
-        narrow = (slice(None), slice(0, head_dim))
         part = (
-            low[0] * low_bits[narrow] + high[0] * high_bits[narrow],
-            low[1] * low_bits[narrow] + high[1] * high_bits[narrow],
+            low[0] * low_bits + high[0] * high_bits,
+            low[1] * low_bits + high[1] * high_bits,
             jnp.where(is_low, low[2], high[2]),
             jnp.where(is_low, low[3], high[3]),
         )
@@ -458,9 +462,14 @@
     def _(g):
         visit([part_of(me, 0, g)], 0, g, diagonal=True)
 
+    send_own(1)
+
     @pl.loop(0, groups)
     def _(g):
         visit([part_of(me, 1, g)], 1, g, diagonal=True)
+
+    for unit in range(groups):
+        pass_near(unit)
 
     def attend_chip(chip):
         def pair(g):
@@ -483,47 +492,58 @@
         arrive(beside, groups + g)
         visit_picked(beside, g)
 
-    for unit in range(units):
+    for unit in range(groups, units):
         pass_near(unit)
+
+    farther = second + (third - second) * middle
+
+    def pass_both(chip, slot):
+        for unit in range(slot * groups, (slot + 1) * groups):
+            pass_on(chip, unit, unit == 0)
 
     @pl.loop(0, chips - 1)
     def _(j):
         chip = first * ((1 - j) * (2 - j) // 2) + second * (j * (2 - j)) + third * (j * (j - 1) // 2)
-        step = middle + j - 1
-        passing = second + (third - second) * step
+        other = 2 * chip + 1 - core
+        arrive_facts(other)
 
         @pl.loop(0, groups)
         def _(g):
-            @pl.when((j >= 1) & (step <= 1))
+            arrive(other, g)
+            attend_chip(chip)(g)
+
+            @pl.when((j == 1) & (g == 0))
             def _():
-                pass_on(passing, g, g == 0)
-
-            arrive(2 * chip + 1 - core, g)
-
-            @pl.when(g == 0)
-            def _():
-                arrive_facts(2 * chip + 1 - core)
-
-            attend_chip(chip)(g)
+                pass_both(farther, 1)
+
+        @pl.when(j == 0)
+        def _():
+            pass_both(farther, 0)
 
         @pl.loop(0, groups)
         def _(g):
-            @pl.when((j >= 1) & (step <= 1))
+            @pl.when((j == 2) & (middle == 0))
             def _():
-                pass_on(passing, groups + g, False)
+                pass_on(third, groups + g, False)
 
             visit_picked(2 * chip + core, g)
-            arrive(2 * chip + 1 - core, groups + g)
-            visit_picked(2 * chip + 1 - core, g)
-
-    @pl.loop(0, 2)
-    def _(row):
-        rows = pl.ds(pl.multiple_of(row * block_len, block_len), block_len)
-        for g in range(groups):
-            for h in range(per_group):
-                start = (g * per_group + h) * head_dim
-                mean = sum_ref[row, g, h] / total_ref[row, g, h : h + 1, :]
-                attended[rows, start : start + head_dim] = mean.astype(attended.dtype).T
+
+            @pl.when((j == 1) & (g == groups - 1) & (middle == 0))
+            def _():
+                pass_both(third, 0)
+
+            arrive(other, groups + g)
+            visit_picked(other, g)
+
+            @pl.when(j == chips - 2)
+            def _():
+                for row in range(2):
+                    for h in range(per_group):
+                        start = pl.multiple_of((g * per_group + h) * head_dim, head_dim)
+                        mean = sum_ref[row, g, h] / total_ref[row, g, h : h + 1, :]
+                        attended[
+                            row * block_len : (row + 1) * block_len, pl.ds(start, head_dim)
+                        ] = mean.astype(attended.dtype).T
 
     def first_copy(c):
         near = along_x + (c % 2) * (along_y - along_x)
@@ -631,7 +651,7 @@
         out_specs=whole,
         scratch_shapes=[
             pltpu.VMEM((devices, units, block_len, width), jnp.bfloat16),
-            pltpu.VMEM((devices, 16, width), jnp.float32),
+            pltpu.VMEM((devices, 16, head_dim), jnp.bfloat16),
             pltpu.VMEM(state + (head_dim, block_len), jnp.bfloat16),
             pltpu.VMEM(state + (block_len,), jnp.float32),
             pltpu.VMEM(state + (block_len,), jnp.float32),

time: 125 us -> 123 us (0.984)
  Pallas kernels: 121 us -> 119 us
    pallas_call x1, Pallas kernels: 121 us -> 119 us  [mix(): pl.pallas_call(functools.partial(mix_kernel, math.log2(math.e) / math.sqr...]
where the time goes in v3:
time: 123 us
  Pallas kernels  119 us (97%)
  local copies, waits for them, and re-layouts  2.06 us (2%)
  other arithmetic  1.73 us (1%)
    pallas_call x1, Pallas kernels, mix(): pl.pallas_call(functools.partial(mix_kernel, math.log2(math.e) / math.sqr...  119 us

profile of v3, /device:TPU:0, one launch (start us, length us, event | category | flops | bytes accessed | tf_op | source)
XLA Modules:
  0.0 122.8 jit_solution(3594405000845970513)
XLA Ops:
  0.0 0.0 copy-start.3
  0.0 1.7 %pad_maximum_fusion = bf16[512,2,256]{2,1,0:T(2,128)(2,1)S(1)} fusion(bf16[512,2,128]{2,1,0:T(2,128)(2,1)} %param.9, bf16[512,2,128]{2,1,0:T(2,128)(2,1)} %param.8), kind=kLoop, calls=%fused_computation.1 | loop fusion | flops 1048576 | bytes 1048576 | tf_op jit(solution)/shard_map/concatenate | solution.py:639
  1.7 0.1 copy.8
  1.8 0.0 copy-done.3
  1.8 0.0 copy-start
  1.8 0.0 copy-start.1
  1.9 0.0 copy-start.2
  1.9 0.5 copy.11
  2.4 0.1 copy-done
  2.5 0.0 copy-done.1
  2.5 0.0 copy-done.2
  2.5 118.9 %shard_map.73 = bf16[128,8192]{1,0:T(8,128)(2,1)S(1)} custom-call(s32[2]{0:T(128)S(1)} %copy-done, bf16[4,256,256]{2,1,0:T(8,128)(2,1)S(1)} %bitcast.9, bf16[2,2]{1,0:T(2,128)(2,1)S(1)} %copy-done.1, bf16[2,2]{1,0:T(2,128)(2,1)S(1)} %copy-done.2, bf16[512,2048]{1,0:T(8,128)(2,1)S(1)} %bitcast.8, bf16[2048,8192]{1,0:T(8,128)(2,1)} %w_ref.1), custom_call_target="tpu_custom_call" | custom-call | flops 26306674688 | bytes 33554432 | tf_op jit(solution)/shard_map/pallas_call | solution.py:644
  121.4 1.3 %copy.13 = bf16[128,8192]{1,0:T(8,128)(2,1)} copy(bf16[128,8192]{1,0:T(8,128)(2,1)S(1)} %shard_map.73) | data formatting | bytes 4194304
Async XLA Ops:
  0.0 1.8 %copy-start.3 = (bf16[512,16,128]{2,1,0:T(8,128)(2,1)S(1)}, bf16[512,16,128]{2,1,0:T(8,128)(2,1)}, u32[]{:S(2)}) copy-start(bf16[512,16,128]{2,1,0:T(8,128)(2,1)} %param.7) | copy-start | bytes 6291460
  1.8 0.7 copy-start
  1.8 0.7 copy-start.1
  1.9 0.7 copy-start.2
